TPU v7x, 32 devices: a whole 2x2x4 slice. The times are simulated.
32 devices in a mesh: dp: 8 (over z, x), seq: 4 (over y, core).
Axes of the slice: x: 2, y: 2, z: 4, core: 2. Of those that a mesh axis runs over, the one named last changes fastest.
Arguments:
- field: bfloat16 [8, 2048, 1024], P('dp', 'seq'), may hold values from -6 to 6
- eq_embed: bfloat16 [8, 512, 1024], P('dp', 'seq'), may hold values from -6 to 6
- eq_len: int32 [8], replicated, may hold values from 1 to 512, 2048 in all
- owner: int32 [8], replicated, may hold values from 0 to 7, as said below
- norm_gain: float32 [1024], replicated, may hold values from 0.1 to 1.9
- w_qkv: bfloat16 [1024, 3072], replicated, may hold values from -0.176776695 to 0.176776695
- w_out: bfloat16 [1024, 1024], replicated, may hold values from -0.1875 to 0.1875
- cross_gain: float32 [1024], replicated, may hold values from 0.1 to 1.9
- w_cq: bfloat16 [1024, 1024], replicated, may hold values from -0.125 to 0.125
- w_ckv: bfloat16 [1024, 2048], replicated, may hold values from -0.125 to 0.125
- w_cout: bfloat16 [1024, 1024], replicated, may hold values from -0.1875 to 0.1875
Outputs:
- joined: bfloat16 [8, 2048, 1024], P('dp', 'seq')
Inputs may be any that keep to these rules, and one draw needn't show every extreme that they name: `owner`: every slot number appears exactly once. `eq_len`: some slot has all 512 tokens real.
All inputs are finite; a program needn't handle non-finite values.
Results may differ from a plain program's by a relative error of at most 0.0055.
Values may be sent and summed in bfloat16 or wider, within the bound.
A program may use at most 128 MiB of HBM per device.

v0:
```python
import jax
import jax.numpy as jnp
from jax import lax
from jax.sharding import PartitionSpec as P

D = 1024
HEADS = 16
HEAD_DIM = 64


def normalize(values, gain):
    return values * lax.rsqrt(jnp.mean(values * values, axis=-1, keepdims=True) + 1e-06) * gain


def attend(query, keys, values, valid):
    rows = query.shape[0]
    heads = query.shape[1]
    depth = query.shape[2]
    block = min(512, rows)
    scale = depth ** (-0.5)

    def one_block(query_block):
        scores = (
            jnp.einsum("qhd,khd->hqk", query_block, keys, preferred_element_type=jnp.float32)
            * scale
        )
        expo = jnp.where(valid[None, None, :], jnp.exp(scores), 0.0)
        weights = (expo / jnp.sum(expo, axis=-1, keepdims=True)).astype(jnp.bfloat16)
        return jnp.einsum(
            "hqk,khd->qhd", weights, values, preferred_element_type=jnp.float32
        ).astype(jnp.bfloat16)

    blocks = lax.map(one_block, query.reshape(rows // block, block, heads, depth))
    return blocks.reshape(rows, heads * depth)


def pick_slot(wanted, carry, piece):
    inside = (wanted >= 0) & (wanted < piece.shape[0])
    picked = lax.dynamic_index_in_dim(
        piece, jnp.clip(wanted, 0, piece.shape[0] - 1), 0, keepdims=False
    )
    return jnp.where(inside, picked, carry)


def per_device(
    field, eq_embed, eq_len, owner, norm_gain, w_qkv, w_out, cross_gain, w_cq, w_ckv, w_cout
):
    tokens = field[0].astype(jnp.float32)
    tok_rows = tokens.shape[0]
    groups = lax.axis_size("seq")
    head_count = HEADS // groups
    normed = normalize(tokens, norm_gain).astype(jnp.bfloat16)
    projected = jnp.dot(normed, w_qkv, preferred_element_type=jnp.float32).astype(jnp.bfloat16)
    stacked = projected.reshape(tok_rows, 3, D)
    local_heads = lax.all_to_all(stacked, "seq", split_axis=2, concat_axis=0, tiled=True)
    seq_rows = local_heads.shape[0]
    split = local_heads.reshape(seq_rows, 3, head_count, HEAD_DIM)
    every = jnp.ones((seq_rows,), dtype=bool)
    attended = attend(split[:, 0], split[:, 1], split[:, 2], every)
    merged = lax.all_to_all(attended, "seq", split_axis=0, concat_axis=1, tiled=True)
    mixed = tokens + jnp.dot(merged, w_out, preferred_element_type=jnp.float32)
    cross_in = normalize(mixed, cross_gain).astype(jnp.bfloat16)
    cross_q = jnp.dot(cross_in, w_cq, preferred_element_type=jnp.float32).astype(jnp.bfloat16)
    slot = lax.dynamic_index_in_dim(owner, lax.axis_index("dp"), 0, keepdims=False)
    length = lax.dynamic_index_in_dim(eq_len, slot, 0, keepdims=False)
    eq_rows = eq_embed.shape[1]
    empty = jnp.zeros(eq_embed.shape[1:], jnp.bfloat16)
    owned_rows = pick_slot(slot, empty, lax.all_gather(eq_embed, "dp", axis=0, tiled=True))
    owned_kv = jnp.dot(owned_rows, w_ckv, preferred_element_type=jnp.float32).astype(jnp.bfloat16)
    whole_kv = lax.all_gather(owned_kv, "seq", axis=0, tiled=True)
    whole_kv = whole_kv.reshape(eq_rows * groups, 2, HEADS, HEAD_DIM)
    valid = jnp.arange(eq_rows * groups, dtype=jnp.int32) < length
    cross_att = attend(
        cross_q.reshape(tok_rows, HEADS, HEAD_DIM), whole_kv[:, 0], whole_kv[:, 1], valid
    )
    joined = mixed + jnp.dot(cross_att, w_cout, preferred_element_type=jnp.float32)
    return joined.astype(jnp.bfloat16)[None]


def solution(mesh):
    in_specs = (
        P("dp", "seq", None),
        P("dp", "seq", None),
        P(),
        P(),
        P(),
        P(),
        P(),
        P(),
        P(),
        P(),
        P(),
    )
    out_specs = P("dp", "seq", None)
    return jax.shard_map(
        per_device, mesh=mesh, in_specs=in_specs, out_specs=out_specs, check_vma=False
    )
```

profile of v0, /device:TPU:0, one launch (start us, length us, event | category | flops | bytes accessed | tf_op | source)
XLA Modules:
  0.0 189.4 jit_solution(14081409868850262506)
XLA Ops:
  8.8 8.3 %convolution_convert_fusion = bf16[512,3072]{1,0:T(8,128)(2,1)} fusion(bf16[1024,3072]{1,0:T(8,128)(2,1)} %param.18, bf16[1,512,1024]{2,1,0:T(8,128)(2,1)} %param.13, f32[1024]{0:T(1024)} %param.17, f32[512]{0:T(512)S(1)} %add_rsqrt_fusion.1), kind=kOutput, calls=%fused_computation.16 | convolution fusion | flops 3224895488 | bytes 10491904 | tf_op jit(solution)/shard_map/dot_general | solution.py:53
  17.1 4.7 %copy.28 = bf16[512,3072]{0,1:T(8,128)(2,1)} copy(bf16[512,3072]{1,0:T(8,128)(2,1)} %convolution_convert_fusion) | data formatting | bytes 6291456 | tf_op jit(solution)/shard_map/convert_element_type | solution.py:53
  21.7 6.5 %copy.29 = bf16[512,3,1024]{0,1,2:T(4,128)(2,1)} copy(bf16[512,3,1024]{0,2,1:T(8,128)(2,1)} %bitcast.75) | data formatting | bytes 6291456 | tf_op jit(solution)/shard_map/reshape | solution.py:54
  28.3 5.0 %all-to-all-start = ((bf16[512,3,1024]{0,1,2:T(4,128)(2,1)}), bf16[512,3,1024]{0,1,2:T(4,128)(2,1)}, u32[]{:S(2)}, u32[]{:S(2)}) async-start(bf16[512,3,1024]{0,1,2:T(4,128)(2,1)} %copy.29), calls=%async_computation | async-start | bytes 8388608 | tf_op jit(solution)/shard_map/all_to_all | solution.py:55
  35.8 46.4 %all-to-all-done = bf16[512,3,1024]{0,1,2:T(4,128)(2,1)} async-done(((bf16[512,3,1024]{0,1,2:T(4,128)(2,1)}), bf16[512,3,1024]{0,1,2:T(4,128)(2,1)}, u32[]{:S(2)}, u32[]{:S(2)}) %all-to-all-start) | async-done | bytes 3145760 | tf_op jit(solution)/shard_map/all_to_all | solution.py:55
  82.2 3.0 %copy.30 = bf16[512,3,1024]{0,2,1:T(8,128)(2,1)S(1)} copy(bf16[512,3,1024]{0,1,2:T(4,128)(2,1)} %all-to-all-done) | data formatting | bytes 6291456 | tf_op jit(solution)/shard_map/all_to_all | solution.py:55
  85.1 4.1 %copy.31 = bf16[4,512,3,256]{1,0,3,2:T(4,128)(2,1)} copy(bf16[4,512,3,256]{1,3,0,2:T(8,128)(2,1)S(1)} %bitcast.76) | data formatting | bytes 6291456 | tf_op jit(solution)/shard_map/all_to_all | solution.py:55
  89.2 6.1 %reshape.50 = bf16[2048,3,4,64]{0,3,2,1:T(8,128)(2,1)} reshape(bf16[4,512,3,256]{1,0,3,2:T(4,128)(2,1)} %copy.31) | data formatting | bytes 6291456 | tf_op jit(solution)/shard_map/reshape | solution.py:57
  95.3 3.6 %slice_bitcast_fusion.4 = (bf16[2048,4,64]{0,2,1:T(8,128)(2,1)}, bf16[2048,4,64]{0,2,1:T(8,128)(2,1)S(1)}, bf16[2048,1,4,64]{0,3,2,1:T(8,128)(2,1)}) fusion(bf16[2048,3,4,64]{0,3,2,1:T(8,128)(2,1)} %reshape.50), kind=kLoop, calls=%fused_computation.33 | loop fusion | bytes 6291456 | tf_op jit(solution)/shard_map/squeeze | solution.py:59
  103.9 3.8 %convolution_convert_fusion.1 = bf16[128,2048]{1,0:T(8,128)(2,1)} fusion(bf16[1024,2048]{1,0:T(8,128)(2,1)} %param.22, bf16[8,128,1024]{2,1,0:T(8,128)(2,1)} %all-gather.3.cloned.1.call-done, s32[]{:T(128)S(6)} %min.4, pred[]{:T(512)S(6)} %and.4), kind=kOutput, calls=%fused_computation.20 | convolution fusion | flops 537264128 | bytes 4980741 | tf_op jit(solution)/shard_map/dot_general | solution.py:69
  107.8 33.5 %while.2 = (s32[]{:T(128)}, bf16[4,512,4,64]{1,3,2,0:T(8,128)(2,1)}, bf16[4,512,4,64]{1,3,2,0:T(8,128)(2,1)}, bf16[2048,4,64]{0,2,1:T(8,128)(2,1)S(1)}, bf16[2048,4,64]{0,2,1:T(8,128)(2,1)}, /*index=5*/s32[]{:T(128)}) while((s32[]{:T(128)}, bf16[4,512,4,64]{1,3,2,0:T(8,128)(2,1)}, bf16[4,512,4,64]{1,3,2,0:T(8,128)(2,1)}, ...), condition=%wide.region_3.4_spmd, body=%wide.region_1.3_spmd.sunk | while | flops 1094842368 | bytes 40386672 | solution.py:33
  107.8 4.0 %fusion.49 = (f32[4,512]{1,0:T(4,128)S(1)}, f32[4,512,2048]{2,1,0:T(8,128)S(1)}) fusion(bf16[2048,4,64]{0,2,1:T(8,128)(2,1)S(1)} %get-tuple-element.135, bf16[4,512,4,64]{1,3,2,0:T(8,128)(2,1)} %get-tuple-element.134, s32[]{:T(128)S(6)} %copy.40), kind=kOutput, calls=%fused_computation.2.clone.1 | convolution fusion | flops 545257472 | bytes 18096132 | tf_op jit(solution)/shard_map/while/body/eval_jaxpr/qhd,khd->hqk/dot_general | solution.py:24
  111.9 4.3 %fusion.50 = bf16[4,512,4,64]{1,3,2,0:T(8,128)(2,1)} fusion(bf16[4,512,4,64]{1,3,2,0:T(8,128)(2,1)} %get-tuple-element.127, s32[]{:T(128)S(6)} %copy.40, bf16[2048,4,64]{0,2,1:T(8,128)(2,1)S(1)} %copy-done.4, f32[4,512,2048]{2,1,0:T(8,128)S(1)} %get-tuple-element.118, f32[4,512]{1,0:T(4,128)S(1)} %get-tuple-element.119), kind=kOutput, calls=%fused_computation.6.clone.1 | convolution fusion | flops 549584896 | bytes 18096132 | tf_op jit(solution)/shard_map/while/body/eval_jaxpr/hqk,khd->qhd/dot_general | solution.py:29
  116.2 4.1 %fusion.49 = (f32[4,512]{1,0:T(4,128)S(1)}, f32[4,512,2048]{2,1,0:T(8,128)S(1)}) fusion(bf16[2048,4,64]{0,2,1:T(8,128)(2,1)S(1)} %get-tuple-element.135, bf16[4,512,4,64]{1,3,2,0:T(8,128)(2,1)} %get-tuple-element.134, s32[]{:T(128)S(6)} %copy.40), kind=kOutput, calls=%fused_computation.2.clone.1 | convolution fusion | flops 545257472 | bytes 18096132 | tf_op jit(solution)/shard_map/while/body/eval_jaxpr/qhd,khd->hqk/dot_general | solution.py:24
  120.3 4.3 %fusion.50 = bf16[4,512,4,64]{1,3,2,0:T(8,128)(2,1)} fusion(bf16[4,512,4,64]{1,3,2,0:T(8,128)(2,1)} %get-tuple-element.127, s32[]{:T(128)S(6)} %copy.40, bf16[2048,4,64]{0,2,1:T(8,128)(2,1)S(1)} %copy-done.4, f32[4,512,2048]{2,1,0:T(8,128)S(1)} %get-tuple-element.118, f32[4,512]{1,0:T(4,128)S(1)} %get-tuple-element.119), kind=kOutput, calls=%fused_computation.6.clone.1 | convolution fusion | flops 549584896 | bytes 18096132 | tf_op jit(solution)/shard_map/while/body/eval_jaxpr/hqk,khd->qhd/dot_general | solution.py:29
  124.6 4.0 %fusion.49 = (f32[4,512]{1,0:T(4,128)S(1)}, f32[4,512,2048]{2,1,0:T(8,128)S(1)}) fusion(bf16[2048,4,64]{0,2,1:T(8,128)(2,1)S(1)} %get-tuple-element.135, bf16[4,512,4,64]{1,3,2,0:T(8,128)(2,1)} %get-tuple-element.134, s32[]{:T(128)S(6)} %copy.40), kind=kOutput, calls=%fused_computation.2.clone.1 | convolution fusion | flops 545257472 | bytes 18096132 | tf_op jit(solution)/shard_map/while/body/eval_jaxpr/qhd,khd->hqk/dot_general | solution.py:24
  128.6 4.3 %fusion.50 = bf16[4,512,4,64]{1,3,2,0:T(8,128)(2,1)} fusion(bf16[4,512,4,64]{1,3,2,0:T(8,128)(2,1)} %get-tuple-element.127, s32[]{:T(128)S(6)} %copy.40, bf16[2048,4,64]{0,2,1:T(8,128)(2,1)S(1)} %copy-done.4, f32[4,512,2048]{2,1,0:T(8,128)S(1)} %get-tuple-element.118, f32[4,512]{1,0:T(4,128)S(1)} %get-tuple-element.119), kind=kOutput, calls=%fused_computation.6.clone.1 | convolution fusion | flops 549584896 | bytes 18096132 | tf_op jit(solution)/shard_map/while/body/eval_jaxpr/hqk,khd->qhd/dot_general | solution.py:29
  132.9 4.0 %fusion.49 = (f32[4,512]{1,0:T(4,128)S(1)}, f32[4,512,2048]{2,1,0:T(8,128)S(1)}) fusion(bf16[2048,4,64]{0,2,1:T(8,128)(2,1)S(1)} %get-tuple-element.135, bf16[4,512,4,64]{1,3,2,0:T(8,128)(2,1)} %get-tuple-element.134, s32[]{:T(128)S(6)} %copy.40), kind=kOutput, calls=%fused_computation.2.clone.1 | convolution fusion | flops 545257472 | bytes 18096132 | tf_op jit(solution)/shard_map/while/body/eval_jaxpr/qhd,khd->hqk/dot_general | solution.py:24
  137.0 4.3 %fusion.50 = bf16[4,512,4,64]{1,3,2,0:T(8,128)(2,1)} fusion(bf16[4,512,4,64]{1,3,2,0:T(8,128)(2,1)} %get-tuple-element.127, s32[]{:T(128)S(6)} %copy.40, bf16[2048,4,64]{0,2,1:T(8,128)(2,1)S(1)} %copy-done.4, f32[4,512,2048]{2,1,0:T(8,128)S(1)} %get-tuple-element.118, f32[4,512]{1,0:T(4,128)S(1)} %get-tuple-element.119), kind=kOutput, calls=%fused_computation.6.clone.1 | convolution fusion | flops 549584896 | bytes 18096132 | tf_op jit(solution)/shard_map/while/body/eval_jaxpr/hqk,khd->qhd/dot_general | solution.py:29
  141.3 3.7 %all-to-all-start.1 = ((bf16[4,512,256]{1,2,0:T(8,128)(2,1)}), bf16[4,512,256]{1,2,0:T(8,128)(2,1)S(1)}, u32[]{:S(2)}, u32[]{:S(2)}) async-start(bf16[4,512,256]{1,2,0:T(8,128)(2,1)} %bitcast.80), calls=%async_computation.1 | async-start | bytes 2097152 | tf_op jit(solution)/shard_map/all_to_all | solution.py:60
  148.0 11.3 %all-to-all-done.1 = bf16[4,512,256]{1,2,0:T(8,128)(2,1)S(1)} async-done(((bf16[4,512,256]{1,2,0:T(8,128)(2,1)}), bf16[4,512,256]{1,2,0:T(8,128)(2,1)S(1)}, u32[]{:S(2)}, u32[]{:S(2)}) %all-to-all-start.1) | async-done | bytes 1048608 | tf_op jit(solution)/shard_map/all_to_all | solution.py:60
  167.1 3.9 %copy.33 = bf16[512,2048]{0,1:T(8,128)(2,1)} copy(bf16[512,2048]{1,0:T(8,128)(2,1)} %all-gather.5.cloned.1.call-done) | data formatting | bytes 4194304 | tf_op jit(solution)/shard_map/all_gather | solution.py:70
  171.0 5.5 %fusion.10 = (f32[16,512]{1,0:T(8,128)S(1)}, f32[16,512,512]{1,2,0:T(8,128)S(1)}) fusion(pred[512]{0:T(512)(128)(4,1)S(1)} %iota_compare_fusion, bf16[512,16,64]{0,2,1:T(8,128)(2,1)S(1)} %bitcast.81, bf16[512,2,16,64]{0,3,2,1:T(8,128)(2,1)} %bitcast.78), kind=kOutput, calls=%fused_computation.14 | convolution fusion | flops 549445632 | bytes 18907648 | tf_op jit(solution)/shard_map/while/body/eval_jaxpr/qhd,khd->hqk/dot_general | solution.py:24
  176.6 3.7 %fusion.15 = bf16[16,64,512]{2,1,0:T(8,128)(2,1)S(1)} fusion(f32[16,512,512]{1,2,0:T(8,128)S(1)} %get-tuple-element.84, f32[16,512]{1,0:T(8,128)S(1)} %get-tuple-element.83, pred[512]{0:T(512)(128)(4,1)S(1)} %iota_compare_fusion, bf16[512,2,16,64]{0,3,2,1:T(8,128)(2,1)S(1)} %bitcast.79), kind=kOutput, calls=%fused_computation.27 | convolution fusion | flops 554172416 | bytes 18907648 | tf_op jit(solution)/shard_map/while/body/eval_jaxpr/hqk,khd->qhd/dot_general | solution.py:29
  (45 shorter events, 19.5 us)
Async XLA Ops:
  6.5 152.7 %copy-start = (bf16[1024,1024]{1,0:T(8,128)(2,1)S(1)}, bf16[1024,1024]{1,0:T(8,128)(2,1)}, u32[]{:S(2)}) copy-start(bf16[1024,1024]{1,0:T(8,128)(2,1)} %param.19) | copy-start | bytes 6291460
  6.5 97.4 %all-gather.3.cloned.1.call-start = ((), (), s32[]{:S(2)}) async-start(), calls=%async_computation.2 | async-start | bytes 2359296 | tf_op jit(solution)/shard_map/all_gather | solution.py:68
  28.3 5.2 %copy-start.8 = (s32[8]{0:T(128)S(1)}, s32[8]{0:T(128)}, u32[]{:S(2)}) copy-start(s32[8]{0:T(128)} %param.16) | copy-start | bytes 100
  28.3 53.9 %all-to-all-start = ((bf16[512,3,1024]{0,1,2:T(4,128)(2,1)}), bf16[512,3,1024]{0,1,2:T(4,128)(2,1)}, u32[]{:S(2)}, u32[]{:S(2)}) async-start(bf16[512,3,1024]{0,1,2:T(4,128)(2,1)} %copy.29), calls=%async_computation | async-start | bytes 8388608 | tf_op jit(solution)/shard_map/all_to_all | solution.py:55
  33.3 133.8 %all-gather.5.cloned.1.call-start = ((), (), s32[]{:S(2)}) async-start(), calls=%async_computation.3 | async-start | bytes 2621440 | tf_op jit(solution)/shard_map/all_gather | solution.py:70
  107.8 38.9 %copy-start.9 = (s32[8]{0:T(128)S(1)}, s32[8]{0:T(128)}, u32[]{:S(2)}) copy-start(s32[8]{0:T(128)} %param.15) | copy-start | bytes 100
  107.8 4.1 %copy-start.4 = (bf16[2048,4,64]{0,2,1:T(8,128)(2,1)S(1)}, bf16[2048,4,64]{0,2,1:T(8,128)(2,1)}, u32[]{:S(2)}) copy-start(bf16[2048,4,64]{0,2,1:T(8,128)(2,1)} %get-tuple-element.136) | copy-start | bytes 3145732 | tf_op jit(solution)/shard_map/while
  116.2 4.1 %copy-start.4 = (bf16[2048,4,64]{0,2,1:T(8,128)(2,1)S(1)}, bf16[2048,4,64]{0,2,1:T(8,128)(2,1)}, u32[]{:S(2)}) copy-start(bf16[2048,4,64]{0,2,1:T(8,128)(2,1)} %get-tuple-element.136) | copy-start | bytes 3145732 | tf_op jit(solution)/shard_map/while
  124.6 4.0 %copy-start.4 = (bf16[2048,4,64]{0,2,1:T(8,128)(2,1)S(1)}, bf16[2048,4,64]{0,2,1:T(8,128)(2,1)}, u32[]{:S(2)}) copy-start(bf16[2048,4,64]{0,2,1:T(8,128)(2,1)} %get-tuple-element.136) | copy-start | bytes 3145732 | tf_op jit(solution)/shard_map/while
  132.9 4.0 %copy-start.4 = (bf16[2048,4,64]{0,2,1:T(8,128)(2,1)S(1)}, bf16[2048,4,64]{0,2,1:T(8,128)(2,1)}, u32[]{:S(2)}) copy-start(bf16[2048,4,64]{0,2,1:T(8,128)(2,1)} %get-tuple-element.136) | copy-start | bytes 3145732 | tf_op jit(solution)/shard_map/while
  141.3 18.0 %all-to-all-start.1 = ((bf16[4,512,256]{1,2,0:T(8,128)(2,1)}), bf16[4,512,256]{1,2,0:T(8,128)(2,1)S(1)}, u32[]{:S(2)}, u32[]{:S(2)}) async-start(bf16[4,512,256]{1,2,0:T(8,128)(2,1)} %bitcast.80), calls=%async_computation.1 | async-start | bytes 2097152 | tf_op jit(solution)/shard_map/all_to_all | solution.py:60
  159.2 4.1 %copy-start.5 = (bf16[1024,1024]{1,0:T(8,128)(2,1)S(1)}, bf16[1024,1024]{1,0:T(8,128)(2,1)}, u32[]{:S(2)}) copy-start(bf16[1024,1024]{1,0:T(8,128)(2,1)} %param.21) | copy-start | bytes 6291460
  159.2 4.1 %copy-start.7 = (f32[1024]{0:T(1024)S(1)}, f32[1024]{0:T(1024)}, u32[]{:S(2)}) copy-start(f32[1024]{0:T(1024)} %param.20) | copy-start | bytes 12292
  162.0 1.3 copy-start.1
  171.0 5.5 %copy-start.3 = (bf16[512,2048]{0,1:T(8,128)(2,1)S(1)}, bf16[512,2048]{0,1:T(8,128)(2,1)}, u32[]{:S(2)}) copy-start(bf16[512,2048]{0,1:T(8,128)(2,1)} %copy.33) | copy-start | bytes 6291460
  176.6 3.8 %copy-start.2 = (f32[512,1024]{1,0:T(8,128)S(1)}, f32[512,1024]{1,0:T(8,128)}, u32[]{:S(2)}) copy-start(f32[512,1024]{1,0:T(8,128)} %copy-done.1) | copy-start | bytes 6291460
  176.6 3.8 %copy-start.6 = (bf16[1024,1024]{1,0:T(8,128)(2,1)S(1)}, bf16[1024,1024]{1,0:T(8,128)(2,1)}, u32[]{:S(2)}) copy-start(bf16[1024,1024]{1,0:T(8,128)(2,1)} %param.23) | copy-start | bytes 6291460
Sparse Core Ops, SparseCore 0:
  9.5 51.9 all-gather.2
  107.9 23.6 all-gather.4
where the time goes:
time: 190 us; the launch traced here: 189 us
  matrix products  62 us (33%)
  waiting for transfers between devices  58.4 us (31%)
  local copies, waits for them, and re-layouts  41 us (22%)
  between operations  16.9 us (9%)
  starting transfers between devices  8.93 us (5%)
  other arithmetic  2.16 us (1%)
    all_to_all x1, waiting for transfers between devices, per_device(): lax.all_to_all(stacked, 'seq', split_axis=2, concat_axis=0, tiled=True)  46.4 us
    dot_general x5, matrix products, one_block(): jnp.einsum('qhd,khd->hqk', query_block, keys, preferred_element_type=jnp....  21.7 us
    dot_general x5, matrix products, one_block(): jnp.einsum('hqk,khd->qhd', weights, values, preferred_element_type=jnp.fl...  20.9 us
    all_to_all x1, waiting for transfers between devices, per_device(): lax.all_to_all(attended, 'seq', split_axis=0, concat_axis=1, tiled=True)  11.3 us
    dot_general x1, matrix products, per_device(): jnp.dot(normed, w_qkv, preferred_element_type=jnp.float32)  8.28 us
    all_to_all x2, local copies, waits for them, and re-layouts, per_device(): lax.all_to_all(stacked, 'seq', split_axis=2, concat_axis=0, tiled=True)  7.07 us
    reshape x1, local copies, waits for them, and re-layouts, per_device(): stacked = projected.reshape(tok_rows, 3, D)  6.53 us
    reshape x1, local copies, waits for them, and re-layouts, per_device(): split = local_heads.reshape(seq_rows, 3, head_count, HEAD_DIM)  6.1 us
  transfers between devices with their start and end apart: 4, of which 2 were waited for; matrix products, arithmetic and copies ran while one was open for 45% of the time, Pallas kernels for 0%

commit v1 on v0

v1 whole, which is shorter than its diff:
```python
import functools
import math
import jax
import jax.numpy as jnp
from jax import lax
from jax.experimental import pallas as pl
from jax.experimental.pallas import tpu as pltpu
from jax.sharding import PartitionSpec as P

D = 1024
HEADS = 16
HEAD_DIM = 64
PAIR = 2 * HEAD_DIM
Q_SCALE = math.log2(math.e) * HEAD_DIM ** (-0.5)
V_SHRINK = 2.0 ** -10
V_GROW = 2.0 ** 10
CHUNKS = 2
MESH = pl.DeviceIdType.MESH


def rms(values, gain):
    return values * lax.rsqrt(jnp.mean(values * values, axis=-1, keepdims=True) + 1e-06) * gain


def dot(a, b):
    return jnp.dot(a, b, preferred_element_type=jnp.float32)


def dot_nt(a, b):
    return lax.dot_general(a, b, (((1,), (1,)), ((), ())), preferred_element_type=jnp.float32)


def low_lanes(rows):
    return lax.broadcasted_iota(jnp.int32, (rows, PAIR), 1) < HEAD_DIM


def finish(even, odd, low):
    total = pltpu.roll(jnp.where(low, odd, even), HEAD_DIM, axis=1)
    return (jnp.where(low, even, odd) * (V_GROW / total)).astype(jnp.bfloat16)


def self_kernel(
    x_ref, gain_ref, w_hbm, out_ref, xn, wbuf, q_s, k_s, v_s, acc, away,
    w_sem, part_send, part_recv, sib_send, sib_recv, fwd_send, fwd_recv, att_send, att_recv,
):
    me = lax.axis_index("seq")
    core = lax.rem(me, 2)
    sib = me + 1 - 2 * core
    part = lax.rem(me + 2, 4)
    rows = x_ref.shape[0]
    half = D // 2
    pairs = half // PAIR
    step = rows // CHUNKS

    loads = []
    for j in range(3):
        cols = pl.ds(pl.multiple_of(core * half + j * D, half), half)
        loads.append(pltpu.make_async_copy(w_hbm.at[:, cols], wbuf.at[j], w_sem.at[j]))
        loads[-1].start()
    barrier = pltpu.get_barrier_semaphore()
    for other in (sib, part):
        pl.semaphore_signal(barrier, inc=1, device_id={"seq": other}, device_id_type=MESH)
    gain = gain_ref[...]
    to_part, to_sib = [], []
    for i in range(CHUNKS):
        here = pl.ds(i * step, step)
        xn[0, here] = rms(x_ref[here].astype(jnp.float32), gain).astype(jnp.bfloat16)
        if i == 0:
            pl.semaphore_wait(barrier, 2)
        to_part.append(pltpu.make_async_remote_copy(
            src_ref=xn.at[0, here], dst_ref=xn.at[2, here],
            send_sem=part_send.at[i], recv_sem=part_recv.at[i],
            device_id={"seq": part}, device_id_type=MESH))
        to_part[-1].start()
        to_sib.append(pltpu.make_async_remote_copy(
            src_ref=xn.at[0, here], dst_ref=xn.at[1, here],
            send_sem=sib_send.at[i], recv_sem=sib_recv.at[i],
            device_id={"seq": sib}, device_id_type=MESH))
        to_sib[-1].start()
    for load in loads:
        load.wait()

    blk = 256
    low = low_lanes(blk)

    def project(slot, with_q):
        @pl.loop(0, rows // blk)
        def _(r):
            at = pl.ds(pl.multiple_of(r * blk, blk), blk)
            x = xn[slot, at]
            if with_q:
                qf = (dot(x, wbuf[0]) * Q_SCALE).astype(jnp.bfloat16)
                q_at = pl.ds(pl.multiple_of(slot * rows + r * blk, blk), blk)
                for p in range(pairs):
                    q_s[p, q_at] = qf[:, p * PAIR:(p + 1) * PAIR]
            kf = dot(x, wbuf[1])
            vf = dot(x, wbuf[2]) * V_SHRINK
            kv_at = pl.ds(pl.multiple_of(slot * rows + r * blk, blk), blk)
            for p in range(pairs):
                kp = kf[:, p * PAIR:(p + 1) * PAIR]
                vp = vf[:, p * PAIR:(p + 1) * PAIR]
                k_s[2 * p, kv_at] = jnp.where(low, kp, 0.0).astype(jnp.bfloat16)
                k_s[2 * p + 1, kv_at] = jnp.where(low, 0.0, kp).astype(jnp.bfloat16)
                v_s[2 * p, kv_at] = jnp.where(low, vp, 1.0).astype(jnp.bfloat16)
                v_s[2 * p + 1, kv_at] = jnp.where(low, 1.0, vp).astype(jnp.bfloat16)

    qblk = 512
    qlow = low_lanes(qblk)

    def piece(p, q_at, key_at):
        q = q_s[p, q_at]
        outs = []
        for h in range(2):
            w = jnp.exp2(dot_nt(q, k_s[2 * p + h, key_at])).astype(jnp.bfloat16)
            outs.append(dot(w, v_s[2 * p + h, key_at]))
        return outs

    project(0, True)
    for copy in to_sib:
        copy.wait_recv()
    project(1, True)

    @pl.loop(0, pairs * 2)
    def _(it):
        p = it // 2
        q_at = pl.ds(pl.multiple_of(lax.rem(it, 2) * qblk, qblk), qblk)
        for n in range(2):
            outs = piece(p, q_at, pl.ds(n * rows, rows))
            for h in range(2):
                if n == 0:
                    acc[2 * p + h, q_at] = outs[h]
                else:
                    acc[2 * p + h, q_at] += outs[h]

    for copy in to_part:
        copy.wait_recv()
    forwards = []
    for i in range(CHUNKS):
        here = pl.ds(i * step, step)
        forwards.append(pltpu.make_async_remote_copy(
            src_ref=xn.at[2, here], dst_ref=xn.at[3, here],
            send_sem=fwd_send.at[i], recv_sem=fwd_recv.at[i],
            device_id={"seq": sib}, device_id_type=MESH))
        forwards[-1].start()
    project(2, False)

    @pl.loop(0, pairs * 2)
    def _(it):
        p = it // 2
        q_at = pl.ds(pl.multiple_of(lax.rem(it, 2) * qblk, qblk), qblk)
        outs = piece(p, q_at, pl.ds(2 * rows, rows))
        for h in range(2):
            acc[2 * p + h, q_at] += outs[h]

    for copy in forwards:
        copy.wait_recv()
    project(3, False)

    def last(p, q_at):
        outs = piece(p, q_at, pl.ds(3 * rows, rows))
        even = acc[2 * p, q_at] + outs[0]
        odd = acc[2 * p + 1, q_at] + outs[1]
        return finish(even, odd, qlow)

    for p in range(pairs):
        away[:, p * PAIR:(p + 1) * PAIR] = last(p, pl.ds(rows, rows))
    back = pltpu.make_async_remote_copy(
        src_ref=away, dst_ref=out_ref.at[core], send_sem=att_send, recv_sem=att_recv,
        device_id={"seq": sib}, device_id_type=MESH)
    back.start()
    for p in range(pairs):
        out_ref[core, :, p * PAIR:(p + 1) * PAIR] = last(p, pl.ds(0, rows))
    back.wait()
    for copy in to_part + to_sib + forwards:
        copy.wait_send()


def self_attention(tokens, gain, w_qkv):
    rows = tokens.shape[0]
    half = D // 2
    vmem = pl.BlockSpec(memory_space=pltpu.VMEM)
    dma = pltpu.SemaphoreType.DMA
    return pl.pallas_call(
        self_kernel,
        name="self_attention",
        out_shape=jax.ShapeDtypeStruct((2, rows, half), jnp.bfloat16),
        in_specs=[vmem, vmem, pl.BlockSpec(memory_space=pl.ANY)],
        out_specs=vmem,
        scratch_shapes=[
            pltpu.VMEM((4, rows, D), jnp.bfloat16),
            pltpu.VMEM((3, D, half), jnp.bfloat16),
            pltpu.VMEM((half // PAIR, 2 * rows, PAIR), jnp.bfloat16),
            pltpu.VMEM((half // HEAD_DIM, 4 * rows, PAIR), jnp.bfloat16),
            pltpu.VMEM((half // HEAD_DIM, 4 * rows, PAIR), jnp.bfloat16),
            pltpu.VMEM((half // HEAD_DIM, 2 * rows, PAIR), jnp.float32),
            pltpu.VMEM((rows, half), jnp.bfloat16),
            dma((3,)),
            dma((CHUNKS,)), dma((CHUNKS,)), dma((CHUNKS,)), dma((CHUNKS,)),
            dma((CHUNKS,)), dma((CHUNKS,)), dma, dma,
        ],
        compiler_params=pltpu.CompilerParams(
            collective_id=0, has_side_effects=True, vmem_limit_bytes=50 << 20),
        cost_estimate=pl.CostEstimate(
            flops=14 * 10 ** 9, bytes_accessed=6 << 20, transcendentals=17 * 10 ** 6),
    )(tokens, gain.reshape(1, D), w_qkv)


def cross_kernel(
    len_ref, att_ref, x_ref, gain_ref, kv_ref, wo_hbm, wq_hbm, wc_hbm, out_ref,
    wo, wq, wc, q_s, mixed, att_s, w_sem,
):
    rows = x_ref.shape[0]
    keys = kv_ref.shape[0]
    half = D // 2
    loads = []
    for j, (src, dst) in enumerate(((wo_hbm, wo), (wq_hbm, wq), (wc_hbm, wc))):
        loads.append(pltpu.make_async_copy(src, dst, w_sem.at[j]))
        loads[-1].start()
    blk = 256
    loads[0].wait()
    loads[1].wait()

    @pl.loop(0, rows // blk)
    def _(r):
        at = pl.ds(pl.multiple_of(r * blk, blk), blk)
        m = (x_ref[at].astype(jnp.float32)
             + dot(att_ref[0, at], wo[:half]) + dot(att_ref[1, at], wo[half:]))
        mixed[at] = m
        cross_in = rms(m, gain_ref[...]).astype(jnp.bfloat16)
        qf = (dot(cross_in, wq[...]) * Q_SCALE).astype(jnp.bfloat16)
        for p in range(HEADS // 2):
            q_s[p, at] = qf[:, p * PAIR:(p + 1) * PAIR]

    low = low_lanes(keys)
    valid = lax.broadcasted_iota(jnp.int32, (keys, PAIR), 0) < len_ref[0]
    qlow = low_lanes(rows)
    one = jnp.where(valid, 1.0, 0.0)
    for p in range(HEADS // 2):
        cols = slice(p * PAIR, (p + 1) * PAIR)
        kp = jnp.where(valid, kv_ref[:, cols].astype(jnp.float32), 0.0)
        vp = jnp.where(valid, kv_ref[:, D + p * PAIR:D + (p + 1) * PAIR].astype(jnp.float32), 0.0)
        vp = vp * V_SHRINK
        q = q_s[p]
        outs = []
        for h in range(2):
            mine = low if h == 0 else jnp.logical_not(low)
            kh = jnp.where(mine, kp, 0.0).astype(jnp.bfloat16)
            vh = jnp.where(mine, vp, one).astype(jnp.bfloat16)
            w = jnp.exp2(dot_nt(q, kh)).astype(jnp.bfloat16)
            outs.append(dot(w, vh))
        att_s[:, cols] = finish(outs[0], outs[1], qlow)

    loads[2].wait()

    @pl.loop(0, rows // blk)
    def _(r):
        at = pl.ds(pl.multiple_of(r * blk, blk), blk)
        out_ref[at] = (mixed[at] + dot(att_s[at], wc[...])).astype(jnp.bfloat16)


def cross_attention(length, att, tokens, gain, kv, w_out, w_cq, w_cout):
    rows = tokens.shape[0]
    vmem = pl.BlockSpec(memory_space=pltpu.VMEM)
    hbm = pl.BlockSpec(memory_space=pl.ANY)
    return pl.pallas_call(
        cross_kernel,
        name="cross_attention",
        out_shape=jax.ShapeDtypeStruct((rows, D), jnp.bfloat16),
        in_specs=[pl.BlockSpec(memory_space=pltpu.SMEM), vmem, vmem, vmem, vmem, hbm, hbm, hbm],
        out_specs=vmem,
        scratch_shapes=[
            pltpu.VMEM((D, D), jnp.bfloat16),
            pltpu.VMEM((D, D), jnp.bfloat16),
            pltpu.VMEM((D, D), jnp.bfloat16),
            pltpu.VMEM((HEADS // 2, rows, PAIR), jnp.bfloat16),
            pltpu.VMEM((rows, D), jnp.float32),
            pltpu.VMEM((rows, D), jnp.bfloat16),
            pltpu.SemaphoreType.DMA((3,)),
        ],
        compiler_params=pltpu.CompilerParams(vmem_limit_bytes=40 << 20),
        cost_estimate=pl.CostEstimate(
            flops=6 * 10 ** 9, bytes_accessed=12 << 20, transcendentals=4 * 10 ** 6),
    )(length, att, tokens, gain.reshape(1, D), kv, w_out, w_cq, w_cout)


def per_device(
    field, eq_embed, eq_len, owner, norm_gain, w_qkv, w_out, cross_gain, w_cq, w_ckv, w_cout
):
    tokens = field[0]
    slot = lax.dynamic_index_in_dim(owner, lax.axis_index("dp"), 0, keepdims=False)
    length = lax.dynamic_slice_in_dim(eq_len, slot, 1, 0)
    slots = lax.all_gather(eq_embed, "dp", axis=0, tiled=True)
    att = self_attention(tokens, norm_gain, w_qkv)
    owned = lax.dynamic_index_in_dim(slots, slot, 0, keepdims=False)
    equation = lax.all_gather(owned, "seq", axis=0, tiled=True)
    kv = jnp.dot(equation, w_ckv, preferred_element_type=jnp.float32).astype(jnp.bfloat16)
    return cross_attention(length, att, tokens, cross_gain, kv, w_out, w_cq, w_cout)[None]


def solution(mesh):
    split = P("dp", "seq", None)
    in_specs = (split, split) + (P(),) * 9
    return jax.shard_map(
        per_device, mesh=mesh, in_specs=in_specs, out_specs=split, check_vma=False
    )
```

time: 190 us -> 136 us (0.72)
  matrix products: 62 us -> 4.99 us
  Pallas kernels: 0 us -> 55.9 us
  local copies, waits for them, and re-layouts: 41 us -> 7.15 us
  starting transfers between devices: 8.93 us -> 0.04 us
  waiting for transfers between devices: 58.4 us -> 51.7 us
  other arithmetic: 2.16 us -> 0 us
    all_to_all x2 -> x0, waiting for transfers between devices: 57.7 us -> none  [the longest x1 46.4 us: per_device(): lax.all_to_all(stacked, 'seq', split_axis=2, concat_axis=0, tiled=True)]
    dot_general x15 -> x1, matrix products: 62 us -> 4.99 us  [per_device(): jnp.dot(equation, w_ckv, preferred_element_type=jnp.float32)]
    pallas_call x0 -> x2, Pallas kernels: none -> 55.9 us  [the longest x1 44.6 us: self_attention(): pl.pallas_call(self_kernel, name='self_attention', out_shape=jax.ShapeDty...]
    all_gather x2, waiting for transfers between devices: 0.02 us -> 51 us  [the longest x1 51 us: per_device(): slots = lax.all_gather(eq_embed, 'dp', axis=0, tiled=True)]
    reshape x2 -> x0, local copies, waits for them, and re-layouts: 12.6 us -> none  [the longest x1 6.53 us: per_device(): stacked = projected.reshape(tok_rows, 3, D)]
    all_to_all x2 -> x0, starting transfers between devices: 8.71 us -> none  [the longest x1 4.97 us: per_device(): lax.all_to_all(stacked, 'seq', split_axis=2, concat_axis=0, tiled=True)]
    all_to_all x2 -> x0, local copies, waits for them, and re-layouts: 7.07 us -> none  [per_device(): lax.all_to_all(stacked, 'seq', split_axis=2, concat_axis=0, tiled=True)]
    convert_element_type x2 -> x0, local copies, waits for them, and re-layouts: 6.18 us -> none  [the longest x1 4.69 us: per_device(): jnp.dot(normed, w_qkv, preferred_element_type=jnp.float32)]
  transfers between devices with their start and end apart: 4 -> 2, of which waited for: 2 -> 1; matrix products, arithmetic and copies ran while one was open for 45% -> 2% of each run, Pallas kernels for 0% -> 33%
where the time goes in v1:
time: 136 us; the launch traced here: 135 us
  Pallas kernels  55.9 us (41%)
  waiting for transfers between devices  51.7 us (38%)
  between operations  15.5 us (11%)
  local copies, waits for them, and re-layouts  7.15 us (5%)
  matrix products  4.99 us (4%)
    all_gather x1, waiting for transfers between devices, per_device(): slots = lax.all_gather(eq_embed, 'dp', axis=0, tiled=True)  51 us
    pallas_call x1, Pallas kernels, self_attention(): pl.pallas_call(self_kernel, name='self_attention', out_shape=jax.ShapeDty...  44.6 us
    pallas_call x1, Pallas kernels, cross_attention(): pl.pallas_call(cross_kernel, name='cross_attention', out_shape=jax.ShapeD...  11.3 us
    dot_general x1, matrix products, per_device(): jnp.dot(equation, w_ckv, preferred_element_type=jnp.float32)  4.99 us
    unnamed x18, local copies, waits for them, and re-layouts  2.91 us
  transfers between devices with their start and end apart: 2, of which 1 were waited for; matrix products, arithmetic and copies ran while one was open for 2% of the time, Pallas kernels for 33%

profile of v1, /device:TPU:0, one launch (start us, length us, event | category | flops | bytes accessed | tf_op | source)
XLA Modules:
  0.0 135.2 jit_solution(16529249067718982555)
XLA Ops:
  6.5 0.0 all-gather.4.cloned.1.call-start
  6.5 0.7 all-gather.4.cloned.1.call-update
  7.3 0.0 all-gather.6.cloned.1.call-start
  7.3 1.2 dynamic_slice.11
  10.5 51.0 %all-gather.4.cloned.1.call-done = bf16[8,128,1024]{2,1,0:T(8,128)(2,1)} async-done(((bf16[1,128,1024]{2,1,0:T(8,128)(2,1)}), bf16[8,128,1024]{2,1,0:T(8,128)(2,1)}) %all-gather.4.cloned.1.call-update) | async-done | bytes 2097168 | tf_op jit(solution)/shard_map/all_gather | solution.py:292
  61.5 1.7 %constant_dynamic-slice_fusion = bf16[1,128,1024]{2,1,0:T(8,128)(2,1)} fusion(bf16[8,128,1024]{2,1,0:T(8,128)(2,1)} %all-gather.4.cloned.1.call-done, s32[]{:T(128)S(6)} %select_n.10), kind=kLoop, calls=%fused_computation.2 | loop fusion | bytes 524292 | tf_op jit(solution)/shard_map/jit(dynamic_index_in_dim)/dynamic_slice | solution.py:294
  63.2 0.0 all-gather.6.cloned.1.call-update
  63.2 1.3 dynamic_slice.12.len_ref
  64.5 1.2 copy-done.3
  65.8 0.7 copy-done.5
  66.4 44.6 %self_attention.1.att_ref = bf16[2,512,512]{2,1,0:T(8,128)(2,1)S(1)} custom-call(bf16[512,1024]{1,0:T(8,128)(2,1)S(1)} %bitcast.9, f32[1,1024]{1,0:T(1,128)S(1)} %bitcast.11, bf16[1024,3072]{1,0:T(8,128)(2,1)} %w_hbm.1), custom_call_target="tpu_custom_call" | custom-call | flops 14000000000 | bytes 6291456 | tf_op jit(solution)/shard_map/self_attention/pallas_call | solution.py:183
  111.0 0.0 copy-start.7
  111.0 1.0 copy-done.7
  112.0 0.0 copy-start.1
  112.0 0.0 copy-start.2
  112.0 0.0 copy-start.8
  112.1 5.0 %convolution_convert_fusion.kv_ref = bf16[512,2048]{1,0:T(8,128)(2,1)S(1)} fusion(bf16[1024,2048]{1,0:T(8,128)(2,1)} %param.20, bf16[1,512,1024]{2,1,0:T(8,128)(2,1)} %all-gather.6.cloned.1.call-done), kind=kOutput, calls=%fused_computation | convolution fusion | flops 2148532224 | bytes 7340032 | tf_op jit(solution)/shard_map/dot_general | solution.py:296
  117.1 0.0 copy-done
  117.1 0.0 copy-done.4
  117.1 0.0 copy-done.6
  117.1 0.0 copy-done.1
  117.1 0.0 copy-done.2
  117.1 0.0 copy-done.8
  117.1 11.3 %cross_attention.1 = bf16[512,1024]{1,0:T(8,128)(2,1)} custom-call(s32[1]{0:T(128)} %dynamic_slice.12.len_ref, bf16[2,512,512]{2,1,0:T(8,128)(2,1)S(1)} %copy-done.8, bf16[512,1024]{1,0:T(8,128)(2,1)S(1)} %bitcast.10, f32[1,1024]{1,0:T(1,128)S(1)} %bitcast.12, bf16[512,2048]{1,0:T(8,128)(2,1)S(1)} %convolution_convert_fusion.kv_ref, ...), custom_call_target="tpu_custom_call" | custom-call | flops 6000000000 | bytes 12582912 | tf_op jit(solution)/shard_map/cross_attention/pallas_call | solution.py:265
  (6 shorter events, 0.0 us)
Async XLA Ops:
  6.5 55.0 %all-gather.4.cloned.1.call-start = ((), (), s32[]{:S(2)}) async-start(), calls=%async_computation | async-start | bytes 2359296 | tf_op jit(solution)/shard_map/all_gather | solution.py:292
  7.3 104.8 %all-gather.6.cloned.1.call-start = ((), (), s32[]{:S(2)}) async-start(), calls=%async_computation.1 | async-start | bytes 1310720 | tf_op jit(solution)/shard_map/all_gather | solution.py:295
  64.5 1.2 copy-start.3
  65.8 0.7 copy-start.5
  111.0 1.0 copy-start.7
  112.0 5.0 %copy-start = (bf16[1024,1024]{1,0:T(8,128)(2,1)S(1)}, bf16[1024,1024]{1,0:T(8,128)(2,1)}, u32[]{:S(2)}) copy-start(bf16[1024,1024]{1,0:T(8,128)(2,1)} %wo_hbm.1) | copy-start | bytes 6291460
  112.0 5.1 %copy-start.4 = (bf16[1,512,1024]{2,1,0:T(8,128)(2,1)S(1)}, bf16[1,512,1024]{2,1,0:T(8,128)(2,1)}, u32[]{:S(2)}) copy-start(bf16[1,512,1024]{2,1,0:T(8,128)(2,1)} %param.11) | copy-start | bytes 3145732
  112.0 5.1 %copy-start.6 = (f32[1024]{0:T(1024)S(1)}, f32[1024]{0:T(1024)}, u32[]{:S(2)}) copy-start(f32[1024]{0:T(1024)} %param.18) | copy-start | bytes 12292
  112.0 5.1 %copy-start.1 = (bf16[1024,1024]{1,0:T(8,128)(2,1)S(1)}, bf16[1024,1024]{1,0:T(8,128)(2,1)}, u32[]{:S(2)}) copy-start(bf16[1024,1024]{1,0:T(8,128)(2,1)} %wq_hbm.1) | copy-start | bytes 6291460
  112.0 5.1 %copy-start.2 = (bf16[1024,1024]{1,0:T(8,128)(2,1)S(1)}, bf16[1024,1024]{1,0:T(8,128)(2,1)}, u32[]{:S(2)}) copy-start(bf16[1024,1024]{1,0:T(8,128)(2,1)} %wc_hbm.1) | copy-start | bytes 6291460
  112.0 5.1 %copy-start.8 = (bf16[2,512,512]{2,1,0:T(8,128)(2,1)S(1)}, bf16[2,512,512]{2,1,0:T(8,128)(2,1)}, u32[]{:S(2)}) copy-start(bf16[2,512,512]{2,1,0:T(8,128)(2,1)} %copy-done.7) | copy-start | bytes 3145732
Sparse Core Ops, SparseCore 0:
  9.5 51.9 all-gather.3
  63.3 20.9 all-gather.5

commit v2 on v1

--- a/solution.py
+++ b/solution.py
@@ -40,9 +40,13 @@
 
 
 def self_kernel(
-    x_ref, gain_ref, w_hbm, out_ref, xn, wbuf, q_s, k_s, v_s, acc, away,
+    owner_ref, x_ref, gain_ref, eq_ref, w_hbm, out_ref, eq_out,
+    xn, wbuf, q_s, k_s, v_s, acc, away, got, picked,
     w_sem, part_send, part_recv, sib_send, sib_recv, fwd_send, fwd_recv, att_send, att_recv,
+    one_send, one_recv, two_send, two_recv, eq_send, eq_recv,
 ):
+    slots = eq_ref.shape[0]
+    my_dp = lax.axis_index("dp")
     me = lax.axis_index("seq")
     core = lax.rem(me, 2)
     sib = me + 1 - 2 * core
@@ -60,13 +64,33 @@
     barrier = pltpu.get_barrier_semaphore()
     for other in (sib, part):
         pl.semaphore_signal(barrier, inc=1, device_id={"seq": other}, device_id_type=MESH)
+
+    @pl.loop(1, slots)
+    def _(i):
+        peer = lax.rem(my_dp + i, slots)
+        pl.semaphore_signal(barrier, inc=1, device_id={"dp": peer}, device_id_type=MESH)
+
+    def scatter(i):
+        peer = lax.rem(my_dp + i, slots)
+        return pltpu.make_async_remote_copy(
+            src_ref=eq_ref.at[peer], dst_ref=got.at[my_dp],
+            send_sem=one_send.at[i], recv_sem=one_recv.at[i],
+            device_id={"dp": peer}, device_id_type=MESH)
+
+    def deliver(i):
+        peer = lax.rem(my_dp + i, slots)
+        return pltpu.make_async_remote_copy(
+            src_ref=picked.at[i], dst_ref=eq_out.at[me, my_dp],
+            send_sem=two_send.at[i], recv_sem=two_recv.at[i],
+            device_id={"dp": peer}, device_id_type=MESH)
+
     gain = gain_ref[...]
     to_part, to_sib = [], []
     for i in range(CHUNKS):
         here = pl.ds(i * step, step)
         xn[0, here] = rms(x_ref[here].astype(jnp.float32), gain).astype(jnp.bfloat16)
         if i == 0:
-            pl.semaphore_wait(barrier, 2)
+            pl.semaphore_wait(barrier, slots + 1)
         to_part.append(pltpu.make_async_remote_copy(
             src_ref=xn.at[0, here], dst_ref=xn.at[2, here],
             send_sem=part_send.at[i], recv_sem=part_recv.at[i],
@@ -77,6 +101,12 @@
             send_sem=sib_send.at[i], recv_sem=sib_recv.at[i],
             device_id={"seq": sib}, device_id_type=MESH))
         to_sib[-1].start()
+
+    @pl.loop(1, slots)
+    def _(i):
+        scatter(i).start()
+
+    got[my_dp] = eq_ref[my_dp]
     for load in loads:
         load.wait()
 
@@ -116,12 +146,22 @@
         return outs
 
     project(0, True)
+
+    @pl.loop(1, slots)
+    def _(i):
+        scatter(i).wait()
+
+    @pl.loop(1, slots)
+    def _(i):
+        picked[i] = got[owner_ref[lax.rem(my_dp + i, slots)]]
+        deliver(i).start()
+
+    eq_out[me, my_dp] = got[owner_ref[my_dp]]
     for copy in to_sib:
         copy.wait_recv()
     project(1, True)
 
-    @pl.loop(0, pairs * 2)
-    def _(it):
+    def local(it):
         p = it // 2
         q_at = pl.ds(pl.multiple_of(lax.rem(it, 2) * qblk, qblk), qblk)
         for n in range(2):
@@ -131,6 +171,24 @@
                     acc[2 * p + h, q_at] = outs[h]
                 else:
                     acc[2 * p + h, q_at] += outs[h]
+
+    pl.loop(0, pairs)(local)
+
+    @pl.loop(1, slots)
+    def _(i):
+        deliver(i).wait()
+
+    eq_part = pltpu.make_async_remote_copy(
+        src_ref=eq_out.at[me], dst_ref=eq_out.at[me],
+        send_sem=eq_send.at[0], recv_sem=eq_recv.at[0],
+        device_id={"seq": part}, device_id_type=MESH)
+    eq_part.start()
+    eq_sib = pltpu.make_async_remote_copy(
+        src_ref=eq_out.at[me], dst_ref=eq_out.at[me],
+        send_sem=eq_send.at[1], recv_sem=eq_recv.at[1],
+        device_id={"seq": sib}, device_id_type=MESH)
+    eq_sib.start()
+    pl.loop(pairs, pairs * 2)(local)
 
     for copy in to_part:
         copy.wait_recv()
@@ -142,6 +200,12 @@
             send_sem=fwd_send.at[i], recv_sem=fwd_recv.at[i],
             device_id={"seq": sib}, device_id_type=MESH))
         forwards[-1].start()
+    eq_part.wait_recv()
+    eq_fwd = pltpu.make_async_remote_copy(
+        src_ref=eq_out.at[part], dst_ref=eq_out.at[part],
+        send_sem=eq_send.at[2], recv_sem=eq_recv.at[2],
+        device_id={"seq": sib}, device_id_type=MESH)
+    eq_fwd.start()
     project(2, False)
 
     @pl.loop(0, pairs * 2)
@@ -171,21 +235,32 @@
     for p in range(pairs):
         out_ref[core, :, p * PAIR:(p + 1) * PAIR] = last(p, pl.ds(0, rows))
     back.wait()
+    eq_part.wait_send()
+    eq_sib.wait()
+    eq_fwd.wait()
     for copy in to_part + to_sib + forwards:
         copy.wait_send()
 
 
-def self_attention(tokens, gain, w_qkv):
+def self_attention(owner, tokens, gain, eq, w_qkv):
     rows = tokens.shape[0]
+    slots = owner.shape[0]
+    pieces = eq.reshape(slots, eq.shape[0] // slots, D)
     half = D // 2
     vmem = pl.BlockSpec(memory_space=pltpu.VMEM)
     dma = pltpu.SemaphoreType.DMA
     return pl.pallas_call(
         self_kernel,
         name="self_attention",
-        out_shape=jax.ShapeDtypeStruct((2, rows, half), jnp.bfloat16),
-        in_specs=[vmem, vmem, pl.BlockSpec(memory_space=pl.ANY)],
-        out_specs=vmem,
+        out_shape=(
+            jax.ShapeDtypeStruct((2, rows, half), jnp.bfloat16),
+            jax.ShapeDtypeStruct((4,) + pieces.shape, jnp.bfloat16),
+        ),
+        in_specs=[
+            pl.BlockSpec(memory_space=pltpu.SMEM), vmem, vmem, vmem,
+            pl.BlockSpec(memory_space=pltpu.HBM),
+        ],
+        out_specs=(vmem, vmem),
         scratch_shapes=[
             pltpu.VMEM((4, rows, D), jnp.bfloat16),
             pltpu.VMEM((3, D, half), jnp.bfloat16),
@@ -194,31 +269,31 @@
             pltpu.VMEM((half // HEAD_DIM, 4 * rows, PAIR), jnp.bfloat16),
             pltpu.VMEM((half // HEAD_DIM, 2 * rows, PAIR), jnp.float32),
             pltpu.VMEM((rows, half), jnp.bfloat16),
+            pltpu.VMEM(pieces.shape, jnp.bfloat16),
+            pltpu.VMEM(pieces.shape, jnp.bfloat16),
             dma((3,)),
             dma((CHUNKS,)), dma((CHUNKS,)), dma((CHUNKS,)), dma((CHUNKS,)),
             dma((CHUNKS,)), dma((CHUNKS,)), dma, dma,
+            dma((slots,)), dma((slots,)), dma((slots,)), dma((slots,)), dma((3,)), dma((3,)),
         ],
         compiler_params=pltpu.CompilerParams(
-            collective_id=0, has_side_effects=True, vmem_limit_bytes=50 << 20),
+            collective_id=0, has_side_effects=True, vmem_limit_bytes=32 << 20),
         cost_estimate=pl.CostEstimate(
             flops=14 * 10 ** 9, bytes_accessed=6 << 20, transcendentals=17 * 10 ** 6),
-    )(tokens, gain.reshape(1, D), w_qkv)
+    )(owner, tokens, gain.reshape(1, D), pieces, w_qkv)
 
 
 def cross_kernel(
-    len_ref, att_ref, x_ref, gain_ref, kv_ref, wo_hbm, wq_hbm, wc_hbm, out_ref,
-    wo, wq, wc, q_s, mixed, att_s, w_sem,
+    len_ref, owner_ref, att_ref, x_ref, gain_ref, eq_ref, wo, wq, wkv, wc, out_ref,
+    q_s, kv_ref, mixed, att_s,
 ):
     rows = x_ref.shape[0]
-    keys = kv_ref.shape[0]
+    keys = eq_ref.shape[0]
     half = D // 2
-    loads = []
-    for j, (src, dst) in enumerate(((wo_hbm, wo), (wq_hbm, wq), (wc_hbm, wc))):
-        loads.append(pltpu.make_async_copy(src, dst, w_sem.at[j]))
-        loads[-1].start()
     blk = 256
-    loads[0].wait()
-    loads[1].wait()
+    for j in range(4):
+        cols = slice(j * half, (j + 1) * half)
+        kv_ref[:, cols] = dot(eq_ref[...], wkv[:, cols]).astype(jnp.bfloat16)
 
     @pl.loop(0, rows // blk)
     def _(r):
@@ -231,8 +306,9 @@
         for p in range(HEADS // 2):
             q_s[p, at] = qf[:, p * PAIR:(p + 1) * PAIR]
 
+    length = len_ref[owner_ref[lax.axis_index("dp")]]
     low = low_lanes(keys)
-    valid = lax.broadcasted_iota(jnp.int32, (keys, PAIR), 0) < len_ref[0]
+    valid = lax.broadcasted_iota(jnp.int32, (keys, PAIR), 0) < length
     qlow = low_lanes(rows)
     one = jnp.where(valid, 1.0, 0.0)
     for p in range(HEADS // 2):
@@ -250,51 +326,40 @@
             outs.append(dot(w, vh))
         att_s[:, cols] = finish(outs[0], outs[1], qlow)
 
-    loads[2].wait()
-
     @pl.loop(0, rows // blk)
     def _(r):
         at = pl.ds(pl.multiple_of(r * blk, blk), blk)
         out_ref[at] = (mixed[at] + dot(att_s[at], wc[...])).astype(jnp.bfloat16)
 
 
-def cross_attention(length, att, tokens, gain, kv, w_out, w_cq, w_cout):
+def cross_attention(eq_len, owner, att, tokens, gain, eq, w_out, w_cq, w_ckv, w_cout):
     rows = tokens.shape[0]
     vmem = pl.BlockSpec(memory_space=pltpu.VMEM)
-    hbm = pl.BlockSpec(memory_space=pl.ANY)
     return pl.pallas_call(
         cross_kernel,
         name="cross_attention",
         out_shape=jax.ShapeDtypeStruct((rows, D), jnp.bfloat16),
-        in_specs=[pl.BlockSpec(memory_space=pltpu.SMEM), vmem, vmem, vmem, vmem, hbm, hbm, hbm],
+        in_specs=[pl.BlockSpec(memory_space=pltpu.SMEM)] * 2 + [vmem] * 8,
         out_specs=vmem,
         scratch_shapes=[
-            pltpu.VMEM((D, D), jnp.bfloat16),
-            pltpu.VMEM((D, D), jnp.bfloat16),
-            pltpu.VMEM((D, D), jnp.bfloat16),
             pltpu.VMEM((HEADS // 2, rows, PAIR), jnp.bfloat16),
+            pltpu.VMEM((eq.shape[0], 2 * D), jnp.bfloat16),
             pltpu.VMEM((rows, D), jnp.float32),
             pltpu.VMEM((rows, D), jnp.bfloat16),
-            pltpu.SemaphoreType.DMA((3,)),
         ],
         compiler_params=pltpu.CompilerParams(vmem_limit_bytes=40 << 20),
         cost_estimate=pl.CostEstimate(
             flops=6 * 10 ** 9, bytes_accessed=12 << 20, transcendentals=4 * 10 ** 6),
-    )(length, att, tokens, gain.reshape(1, D), kv, w_out, w_cq, w_cout)
+    )(eq_len, owner, att, tokens, gain.reshape(1, D), eq, w_out, w_cq, w_ckv, w_cout)
 
 
 def per_device(
     field, eq_embed, eq_len, owner, norm_gain, w_qkv, w_out, cross_gain, w_cq, w_ckv, w_cout
 ):
     tokens = field[0]
-    slot = lax.dynamic_index_in_dim(owner, lax.axis_index("dp"), 0, keepdims=False)
-    length = lax.dynamic_slice_in_dim(eq_len, slot, 1, 0)
-    slots = lax.all_gather(eq_embed, "dp", axis=0, tiled=True)
-    att = self_attention(tokens, norm_gain, w_qkv)
-    owned = lax.dynamic_index_in_dim(slots, slot, 0, keepdims=False)
-    equation = lax.all_gather(owned, "seq", axis=0, tiled=True)
-    kv = jnp.dot(equation, w_ckv, preferred_element_type=jnp.float32).astype(jnp.bfloat16)
-    return cross_attention(length, att, tokens, cross_gain, kv, w_out, w_cq, w_cout)[None]
+    att, eq = self_attention(owner, tokens, norm_gain, eq_embed[0], w_qkv)
+    return cross_attention(
+        eq_len, owner, att, tokens, cross_gain, eq.reshape(-1, D), w_out, w_cq, w_ckv, w_cout)[None]
 
 
 def solution(mesh):

time: 136 us -> 71.1 us (0.52)
  waiting for transfers between devices: 51.7 us -> 0 us
  between operations: 15.5 us -> 0.11 us
  Pallas kernels: 55.9 us -> 64.4 us
  matrix products: 4.99 us -> 0 us
    all_gather x2 -> x0, waiting for transfers between devices: 51 us -> none  [the longest x1 51 us: per_device(): slots = lax.all_gather(eq_embed, 'dp', axis=0, tiled=True)]
    pallas_call x1, Pallas kernels: 44.6 us -> 51.2 us  [self_attention(): pl.pallas_call(self_kernel, name='self_attention', out_shape=(jax.ShapeDt...]
    dot_general x1 -> x0, matrix products: 4.99 us -> none  [per_device(): jnp.dot(equation, w_ckv, preferred_element_type=jnp.float32)]
    dynamic_slice x3 -> x0, local copies, waits for them, and re-layouts: 4.24 us -> none  [the longest x1 1.68 us: per_device(): owned = lax.dynamic_index_in_dim(slots, slot, 0, keepdims=False)]
    unnamed x18 -> x26, local copies, waits for them, and re-layouts: 2.91 us -> 6.33 us
    pallas_call x1, Pallas kernels: 11.3 us -> 13.2 us  [cross_attention(): pl.pallas_call(cross_kernel, name='cross_attention', out_shape=jax.ShapeD...]
  transfers between devices with their start and end apart: 2 -> 0, of which waited for: 1 -> 0; matrix products, arithmetic and copies ran while one was open for 2% -> 0% of each run, Pallas kernels for 33% -> 0%
where the time goes in v2:
time: 71.1 us; the launch traced here: 70.8 us
  Pallas kernels  64.4 us (91%)
  local copies, waits for them, and re-layouts  6.33 us (9%)
    pallas_call x1, Pallas kernels, self_attention(): pl.pallas_call(self_kernel, name='self_attention', out_shape=(jax.ShapeDt...  51.2 us
    pallas_call x1, Pallas kernels, cross_attention(): pl.pallas_call(cross_kernel, name='cross_attention', out_shape=jax.ShapeD...  13.2 us
    unnamed x26, local copies, waits for them, and re-layouts  6.33 us

profile of v2, /device:TPU:0, one launch (start us, length us, event | category | flops | bytes accessed | tf_op | source)
XLA Modules:
  0.0 70.8 jit_solution(6352521820896023771)
XLA Ops:
  0.0 0.0 copy-start
  0.0 2.8 %copy-done = bf16[1024,3072]{1,0:T(8,128)(2,1)S(1)} copy-done((bf16[1024,3072]{1,0:T(8,128)(2,1)S(1)}, bf16[1024,3072]{1,0:T(8,128)(2,1)}, u32[]{:S(2)}) %copy-start) | copy-done | bytes 6291480
  2.8 0.0 copy-start.5
  2.8 1.2 %copy-done.5 = bf16[1,512,1024]{2,1,0:T(8,128)(2,1)S(1)} copy-done((bf16[1,512,1024]{2,1,0:T(8,128)(2,1)S(1)}, bf16[1,512,1024]{2,1,0:T(8,128)(2,1)}, u32[]{:S(2)}) %copy-start.5) | copy-done | bytes 1048600
  4.0 0.0 copy-start.7
  4.0 0.9 %copy-done.7 = bf16[1,128,1024]{2,1,0:T(8,128)(2,1)S(1)} copy-done((bf16[1,128,1024]{2,1,0:T(8,128)(2,1)S(1)}, bf16[1,128,1024]{2,1,0:T(8,128)(2,1)}, u32[]{:S(2)}) %copy-start.7) | copy-done | bytes 262168
  5.0 0.0 copy-start.8
  5.0 0.7 copy-done.8
  5.6 0.0 copy-start.11
  5.7 0.7 copy-done.11
  6.3 0.0 copy-start.6
  6.3 0.0 copy-start.9
  6.3 0.0 copy-start.10
  6.3 0.0 copy-start.12
  6.4 51.2 %self_attention.1 = (bf16[2,512,512]{2,1,0:T(8,128)(2,1)S(1)}, bf16[4,8,16,1024]{3,2,1,0:T(8,128)(2,1)S(1)}) custom-call(s32[8]{0:T(128)S(1)} %copy-done.11, bf16[512,1024]{1,0:T(8,128)(2,1)S(1)} %bitcast.6, f32[1,1024]{1,0:T(1,128)S(1)} %bitcast.9, bf16[8,16,1024]{2,1,0:T(8,128)(2,1)S(1)} %bitcast.8, bf16[1024,3072]{1,0:T(8,128)(2,1)S(1)} %copy-done), custom_call_target="tpu_custom_call" | custom-call | flops 14000000000 | bytes 6291456 | tf_op jit(solution)/shard_map/self_attention/pallas_call | solution.py:252
  57.6 0.0 copy-done.1
  57.6 0.0 copy-done.2
  57.6 0.0 copy-done.3
  57.6 0.0 copy-done.4
  57.6 0.0 copy-done.6
  57.6 0.0 copy-done.9
  57.6 0.0 copy-done.10
  57.6 0.0 copy-done.12
  57.6 13.2 %cross_attention.1 = bf16[512,1024]{1,0:T(8,128)(2,1)} custom-call(s32[8]{0:T(128)S(1)} %copy-done.10, s32[8]{0:T(128)S(1)} %copy-done.12, bf16[2,512,512]{2,1,0:T(8,128)(2,1)S(1)} %get-tuple-element.7.att_ref, bf16[512,1024]{1,0:T(8,128)(2,1)S(1)} %bitcast.7, f32[1,1024]{1,0:T(1,128)S(1)} %bitcast.10, bf16[512,1024]{1,0:T(8,128)(2,1)S(1)} %bitcast.11, ...), custom_call_target="tpu_custom_call" | custom-call | flops 6000000000 | bytes 12582912 | tf_op jit(solution)/shard_map/cross_attention/pallas_call | solution.py:338
  (4 shorter events, 0.0 us)
Async XLA Ops:
  0.0 2.8 %copy-start = (bf16[1024,3072]{1,0:T(8,128)(2,1)S(1)}, bf16[1024,3072]{1,0:T(8,128)(2,1)}, u32[]{:S(2)}) copy-start(bf16[1024,3072]{1,0:T(8,128)(2,1)} %w_hbm.1) | copy-start | bytes 18874372
  2.8 1.2 %copy-start.5 = (bf16[1,512,1024]{2,1,0:T(8,128)(2,1)S(1)}, bf16[1,512,1024]{2,1,0:T(8,128)(2,1)}, u32[]{:S(2)}) copy-start(bf16[1,512,1024]{2,1,0:T(8,128)(2,1)} %param.11) | copy-start | bytes 3145732
  4.0 0.9 %copy-start.7 = (bf16[1,128,1024]{2,1,0:T(8,128)(2,1)S(1)}, bf16[1,128,1024]{2,1,0:T(8,128)(2,1)}, u32[]{:S(2)}) copy-start(bf16[1,128,1024]{2,1,0:T(8,128)(2,1)} %param.12) | copy-start | bytes 786436
  5.0 0.7 copy-start.8
  5.6 0.7 copy-start.11
  6.3 51.3 %copy-start.1 = (bf16[1024,2048]{1,0:T(8,128)(2,1)S(1)}, bf16[1024,2048]{1,0:T(8,128)(2,1)}, u32[]{:S(2)}) copy-start(bf16[1024,2048]{1,0:T(8,128)(2,1)} %wkv.1) | copy-start | bytes 12582916
  6.3 51.3 %copy-start.2 = (bf16[1024,1024]{1,0:T(8,128)(2,1)S(1)}, bf16[1024,1024]{1,0:T(8,128)(2,1)}, u32[]{:S(2)}) copy-start(bf16[1024,1024]{1,0:T(8,128)(2,1)} %wo.1) | copy-start | bytes 6291460
  6.3 51.3 %copy-start.3 = (bf16[1024,1024]{1,0:T(8,128)(2,1)S(1)}, bf16[1024,1024]{1,0:T(8,128)(2,1)}, u32[]{:S(2)}) copy-start(bf16[1024,1024]{1,0:T(8,128)(2,1)} %wq.1) | copy-start | bytes 6291460
  6.3 51.3 %copy-start.4 = (bf16[1024,1024]{1,0:T(8,128)(2,1)S(1)}, bf16[1024,1024]{1,0:T(8,128)(2,1)}, u32[]{:S(2)}) copy-start(bf16[1024,1024]{1,0:T(8,128)(2,1)} %wc.1) | copy-start | bytes 6291460
  6.3 51.3 %copy-start.6 = (bf16[1,512,1024]{2,1,0:T(8,128)(2,1)S(1)}, bf16[1,512,1024]{2,1,0:T(8,128)(2,1)}, u32[]{:S(2)}) copy-start(bf16[1,512,1024]{2,1,0:T(8,128)(2,1)} %param.11) | copy-start | bytes 3145732
  6.3 51.3 %copy-start.9 = (f32[1024]{0:T(1024)S(1)}, f32[1024]{0:T(1024)}, u32[]{:S(2)}) copy-start(f32[1024]{0:T(1024)} %param.18) | copy-start | bytes 12292
  6.3 51.3 %copy-start.10 = (s32[8]{0:T(128)S(1)}, s32[8]{0:T(128)}, u32[]{:S(2)}) copy-start(s32[8]{0:T(128)} %len_ref.1) | copy-start | bytes 100
  6.3 51.3 %copy-start.12 = (s32[8]{0:T(128)S(1)}, s32[8]{0:T(128)}, u32[]{:S(2)}) copy-start(s32[8]{0:T(128)} %owner_ref.3) | copy-start | bytes 100

commit v3 on v0

v3 whole, which is shorter than its diff:
```python
import math
import jax
import jax.numpy as jnp
from jax import lax
from jax.experimental import pallas as pl
from jax.experimental.pallas import tpu as pltpu
from jax.sharding import PartitionSpec as P

D = 1024
HEADS = 16
HEAD_DIM = 64
PAIR = 2 * HEAD_DIM
Q_SCALE = math.log2(math.e) * HEAD_DIM ** (-0.5)
V_SHRINK = 2.0 ** -10
V_GROW = 2.0 ** 10
CHUNKS = 2
MESH = pl.DeviceIdType.MESH


def rms(values, gain):
    return values * lax.rsqrt(jnp.mean(values * values, axis=-1, keepdims=True) + 1e-06) * gain


def dot(a, b):
    return jnp.dot(a, b, preferred_element_type=jnp.float32)


def dot_nt(a, b):
    return lax.dot_general(a, b, (((1,), (1,)), ((), ())), preferred_element_type=jnp.float32)


def low_lanes(rows):
    return lax.broadcasted_iota(jnp.int32, (rows, PAIR), 1) < HEAD_DIM


def finish(even, odd, low):
    total = pltpu.roll(jnp.where(low, odd, even), HEAD_DIM, axis=1)
    return (jnp.where(low, even, odd) * (V_GROW / total)).astype(jnp.bfloat16)


def kernel(
    owner_ref, len_ref, x_hbm, gain_hbm, cross_gain_hbm, eq_hbm,
    w_hbm, wo_hbm, wq_hbm, wkv_hbm, wc_hbm, out_ref,
    x_ref, gains, eq_ref, wbuf, wo, wq, wkv, wc,
    xn, q_s, k_s, v_s, acc, away, att, got, picked, eq_out, cross_q, kv_s, mixed, cross_att,
    x_sem, g_sem, e_sem, w_sem,
    part_send, part_recv, sib_send, sib_recv, fwd_send, fwd_recv, att_send, att_recv,
    one_send, one_recv, two_send, two_recv, eq_send, eq_recv,
):
    slots = eq_ref.shape[0]
    my_dp = lax.axis_index("dp")
    me = lax.axis_index("seq")
    core = lax.rem(me, 2)
    sib = me + 1 - 2 * core
    part = lax.rem(me + 2, 4)
    rows = x_ref.shape[0]
    half = D // 2
    pairs = half // PAIR
    step = rows // CHUNKS

    def load(src, dst, sem):
        copy = pltpu.make_async_copy(src, dst, sem)
        copy.start()
        return copy

    x_loads = []
    for i in range(CHUNKS):
        here = pl.ds(i * step, step)
        x_loads.append(load(x_hbm.at[here], x_ref.at[here], x_sem.at[i]))
        if i == 0:
            gain_load = load(gain_hbm, gains.at[0], g_sem.at[0])
    eq_load = load(eq_hbm, eq_ref, e_sem)
    w_loads = []
    for j in range(3):
        cols = pl.ds(pl.multiple_of(core * half + j * D, half), half)
        w_loads.append(load(w_hbm.at[:, cols], wbuf.at[j], w_sem.at[j]))
    cross_gain_load = load(cross_gain_hbm, gains.at[1], g_sem.at[1])
    late = [
        load(src, dst, w_sem.at[3 + j])
        for j, (src, dst) in enumerate(((wkv_hbm, wkv), (wo_hbm, wo), (wq_hbm, wq), (wc_hbm, wc)))
    ]

    barrier = pltpu.get_barrier_semaphore()
    for other in (sib, part):
        pl.semaphore_signal(barrier, inc=1, device_id={"seq": other}, device_id_type=MESH)

    @pl.loop(1, slots)
    def _(i):
        peer = lax.rem(my_dp + i, slots)
        pl.semaphore_signal(barrier, inc=1, device_id={"dp": peer}, device_id_type=MESH)

    def scatter(i):
        peer = lax.rem(my_dp + i, slots)
        return pltpu.make_async_remote_copy(
            src_ref=eq_ref.at[peer], dst_ref=got.at[my_dp],
            send_sem=one_send.at[i], recv_sem=one_recv.at[i],
            device_id={"dp": peer}, device_id_type=MESH)

    def deliver(i):
        peer = lax.rem(my_dp + i, slots)
        return pltpu.make_async_remote_copy(
            src_ref=picked.at[i], dst_ref=eq_out.at[me, my_dp],
            send_sem=two_send.at[i], recv_sem=two_recv.at[i],
            device_id={"dp": peer}, device_id_type=MESH)

    def push(src, dst, send, recv, other):
        copy = pltpu.make_async_remote_copy(
            src_ref=src, dst_ref=dst, send_sem=send, recv_sem=recv,
            device_id={"seq": other}, device_id_type=MESH)
        copy.start()
        return copy

    gain_load.wait()
    gain = gains[0]
    to_part, to_sib = [], []
    for i in range(CHUNKS):
        here = pl.ds(i * step, step)
        x_loads[i].wait()
        xn[0, here] = rms(x_ref[here].astype(jnp.float32), gain).astype(jnp.bfloat16)
        if i == 0:
            pl.semaphore_wait(barrier, slots + 1)
        to_part.append(
            push(xn.at[0, here], xn.at[2, here], part_send.at[i], part_recv.at[i], part))
        to_sib.append(
            push(xn.at[0, here], xn.at[1, here], sib_send.at[i], sib_recv.at[i], sib))
    eq_load.wait()

    @pl.loop(1, slots)
    def _(i):
        scatter(i).start()

    got[my_dp] = eq_ref[my_dp]
    for copy in w_loads:
        copy.wait()

    low = low_lanes(step)

    def project(slot, i, with_q):
        at = pl.ds(i * step, step)
        x = xn[slot, at]
        key_at = pl.ds(slot * rows + i * step, step)
        if with_q:
            qf = (dot(x, wbuf[0]) * Q_SCALE).astype(jnp.bfloat16)
            for p in range(pairs):
                q_s[p, key_at] = qf[:, p * PAIR:(p + 1) * PAIR]
        kf = dot(x, wbuf[1])
        vf = dot(x, wbuf[2]) * V_SHRINK
        for p in range(pairs):
            kp = kf[:, p * PAIR:(p + 1) * PAIR]
            vp = vf[:, p * PAIR:(p + 1) * PAIR]
            k_s[2 * p, key_at] = jnp.where(low, kp, 0.0).astype(jnp.bfloat16)
            k_s[2 * p + 1, key_at] = jnp.where(low, 0.0, kp).astype(jnp.bfloat16)
            v_s[2 * p, key_at] = jnp.where(low, vp, 1.0).astype(jnp.bfloat16)
            v_s[2 * p + 1, key_at] = jnp.where(low, 1.0, vp).astype(jnp.bfloat16)

    def piece(p, h, q_at, key_at):
        w = jnp.exp2(dot_nt(q_s[p, q_at], k_s[2 * p + h, key_at])).astype(jnp.bfloat16)
        return dot(w, v_s[2 * p + h, key_at])

    every = pl.ds(0, 2 * rows)

    for i in range(CHUNKS):
        project(0, i, True)

    @pl.loop(1, slots)
    def _(i):
        scatter(i).wait()

    @pl.loop(1, slots)
    def _(i):
        picked[i] = got[owner_ref[lax.rem(my_dp + i, slots)]]
        deliver(i).start()

    eq_out[me, my_dp] = got[owner_ref[my_dp]]
    for i in range(CHUNKS):
        to_sib[i].wait_recv()
        project(1, i, True)

    def local(p):
        for h in range(2):
            acc[2 * p + h] = piece(p, h, every, pl.ds(0, rows))
        for h in range(2):
            acc[2 * p + h] += piece(p, h, every, pl.ds(rows, rows))

    pl.loop(0, pairs // 2)(local)

    @pl.loop(1, slots)
    def _(i):
        deliver(i).wait()

    mine = eq_out.at[me]
    eq_part = push(mine, mine, eq_send.at[0], eq_recv.at[0], part)
    eq_sib = push(mine, mine, eq_send.at[1], eq_recv.at[1], sib)
    pl.loop(pairs // 2, pairs)(local)

    forwards = []
    for i in range(CHUNKS):
        here = pl.ds(i * step, step)
        to_part[i].wait_recv()
        forwards.append(
            push(xn.at[2, here], xn.at[3, here], fwd_send.at[i], fwd_recv.at[i], sib))
        for slot in (2, 3):
            if slot == 3:
                if i == CHUNKS - 1:
                    eq_part.wait_recv()
                    theirs = eq_out.at[part]
                    eq_fwd = push(theirs, theirs, eq_send.at[2], eq_recv.at[2], sib)
                forwards[i].wait_recv()
            project(slot, i, False)
            key_at = pl.ds(slot * rows + i * step, step)
            if slot == 3 and i == CHUNKS - 1:
                break

            @pl.loop(0, pairs)
            def _(p):
                for h in range(2):
                    acc[2 * p + h] += piece(p, h, every, key_at)

    qlow = low_lanes(rows)

    def last(p, q_at):
        even = acc[2 * p, q_at] + piece(p, 0, q_at, key_at)
        odd = acc[2 * p + 1, q_at] + piece(p, 1, q_at, key_at)
        return finish(even, odd, qlow)

    for p in range(pairs):
        away[:, p * PAIR:(p + 1) * PAIR] = last(p, pl.ds(rows, rows))
    back = push(away, att.at[core], att_send, att_recv, sib)
    for p in range(pairs):
        att[core, :, p * PAIR:(p + 1) * PAIR] = last(p, pl.ds(0, rows))

    eq_part.wait_send()
    eq_sib.wait()
    eq_fwd.wait()
    cross_gain_load.wait()
    for copy in late:
        copy.wait()
    keys = kv_s.shape[0]
    equation = eq_out[...].reshape(keys, D)
    for j in range(4):
        cols = slice(j * half, (j + 1) * half)
        kv_s[:, cols] = dot(equation, wkv[:, cols]).astype(jnp.bfloat16)
    back.wait()
    for copy in to_part + to_sib + forwards:
        copy.wait_send()

    @pl.loop(0, CHUNKS)
    def _(r):
        at = pl.ds(pl.multiple_of(r * step, step), step)
        m = (x_ref[at].astype(jnp.float32)
             + dot(att[0, at], wo[:half]) + dot(att[1, at], wo[half:]))
        mixed[at] = m
        cross_in = rms(m, gains[1]).astype(jnp.bfloat16)
        qf = (dot(cross_in, wq[...]) * Q_SCALE).astype(jnp.bfloat16)
        for p in range(HEADS // 2):
            cross_q[p, at] = qf[:, p * PAIR:(p + 1) * PAIR]

    length = len_ref[owner_ref[my_dp]]
    klow = low_lanes(keys)
    valid = lax.broadcasted_iota(jnp.int32, (keys, PAIR), 0) < length
    one = jnp.where(valid, 1.0, 0.0)
    for p in range(HEADS // 2):
        cols = slice(p * PAIR, (p + 1) * PAIR)
        kp = jnp.where(valid, kv_s[:, cols].astype(jnp.float32), 0.0)
        vp = jnp.where(valid, kv_s[:, D + p * PAIR:D + (p + 1) * PAIR].astype(jnp.float32), 0.0)
        vp = vp * V_SHRINK
        outs = []
        for h in range(2):
            own = klow if h == 0 else jnp.logical_not(klow)
            kh = jnp.where(own, kp, 0.0).astype(jnp.bfloat16)
            vh = jnp.where(own, vp, one).astype(jnp.bfloat16)
            w = jnp.exp2(dot_nt(cross_q[p], kh)).astype(jnp.bfloat16)
            outs.append(dot(w, vh))
        cross_att[:, cols] = finish(outs[0], outs[1], qlow)

    @pl.loop(0, CHUNKS)
    def _(r):
        at = pl.ds(pl.multiple_of(r * step, step), step)
        out_ref[at] = (mixed[at] + dot(cross_att[at], wc[...])).astype(jnp.bfloat16)


def per_device(
    field, eq_embed, eq_len, owner, norm_gain, w_qkv, w_out, cross_gain, w_cq, w_ckv, w_cout
):
    tokens = field[0]
    rows = tokens.shape[0]
    half = D // 2
    slots = owner.shape[0]
    pieces = eq_embed.reshape(slots, eq_embed.shape[1] // slots, D)
    groups = lax.axis_size("seq")
    keys = groups * eq_embed.shape[1]
    any_space = pl.BlockSpec(memory_space=pl.ANY)
    smem = pl.BlockSpec(memory_space=pltpu.SMEM)
    dma = pltpu.SemaphoreType.DMA
    bf16 = lambda *shape: pltpu.VMEM(shape, jnp.bfloat16)
    f32 = lambda *shape: pltpu.VMEM(shape, jnp.float32)
    chunk_sem = dma((CHUNKS,))
    slot_sem = dma((slots,))
    joined = pl.pallas_call(
        kernel,
        name="joining_layer",
        out_shape=jax.ShapeDtypeStruct((rows, D), jnp.bfloat16),
        in_specs=[smem] * 2 + [any_space] * 9,
        out_specs=pl.BlockSpec(memory_space=pltpu.VMEM),
        scratch_shapes=[
            bf16(rows, D), f32(2, 1, D), bf16(*pieces.shape), bf16(3, D, half),
            bf16(D, D), bf16(D, D), bf16(D, 2 * D), bf16(D, D),
            bf16(groups, rows, D),
            bf16(half // PAIR, 2 * rows, PAIR),
            bf16(half // HEAD_DIM, groups * rows, PAIR),
            bf16(half // HEAD_DIM, groups * rows, PAIR),
            f32(half // HEAD_DIM, 2 * rows, PAIR),
            bf16(rows, half), bf16(2, rows, half),
            bf16(*pieces.shape), bf16(*pieces.shape), bf16(groups, *pieces.shape),
            bf16(HEADS // 2, rows, PAIR), bf16(keys, 2 * D), f32(rows, D), bf16(rows, D),
            chunk_sem, dma((2,)), dma, dma((7,)),
            chunk_sem, chunk_sem, chunk_sem, chunk_sem, chunk_sem, chunk_sem, dma, dma,
            slot_sem, slot_sem, slot_sem, slot_sem, dma((3,)), dma((3,)),
        ],
        compiler_params=pltpu.CompilerParams(
            collective_id=0, has_side_effects=True, vmem_limit_bytes=60 << 20),
        cost_estimate=pl.CostEstimate(
            flops=20 * 10 ** 9, bytes_accessed=16 << 20, transcendentals=21 * 10 ** 6),
    )(
        owner, eq_len, tokens, norm_gain.reshape(1, D), cross_gain.reshape(1, D), pieces,
        w_qkv, w_out, w_cq, w_ckv, w_cout,
    )
    return joined[None]


def solution(mesh):
    split = P("dp", "seq", None)
    in_specs = (split, split) + (P(),) * 9
    return jax.shard_map(
        per_device, mesh=mesh, in_specs=in_specs, out_specs=split, check_vma=False
    )
```

time: 190 us -> 58.3 us (0.31)
  matrix products: 62 us -> 0 us
  waiting for transfers between devices: 58.4 us -> 0 us
  Pallas kernels: 0 us -> 55.8 us
  local copies, waits for them, and re-layouts: 41 us -> 2.26 us
  between operations: 16.9 us -> 0.01 us
  starting transfers between devices: 8.93 us -> 0 us
  other arithmetic: 2.16 us -> 0 us
    dot_general x15 -> x0, matrix products: 62 us -> none  [the longest x5 21.7 us: one_block(): jnp.einsum('qhd,khd->hqk', query_block, keys, preferred_element_type=jnp....]
    all_to_all x2 -> x0, waiting for transfers between devices: 57.7 us -> none  [the longest x1 46.4 us: per_device(): lax.all_to_all(stacked, 'seq', split_axis=2, concat_axis=0, tiled=True)]
    pallas_call x0 -> x1, Pallas kernels: none -> 55.8 us  [per_device(): pl.pallas_call(kernel, name='joining_layer', out_shape=jax.ShapeDtypeStru...]
    reshape x2 -> x0, local copies, waits for them, and re-layouts: 12.6 us -> none  [the longest x1 6.53 us: per_device(): stacked = projected.reshape(tok_rows, 3, D)]
    all_to_all x2 -> x0, starting transfers between devices: 8.71 us -> none  [the longest x1 4.97 us: per_device(): lax.all_to_all(stacked, 'seq', split_axis=2, concat_axis=0, tiled=True)]
    all_to_all x2 -> x0, local copies, waits for them, and re-layouts: 7.07 us -> none  [per_device(): lax.all_to_all(stacked, 'seq', split_axis=2, concat_axis=0, tiled=True)]
    convert_element_type x2 -> x0, local copies, waits for them, and re-layouts: 6.18 us -> none  [the longest x1 4.69 us: per_device(): jnp.dot(normed, w_qkv, preferred_element_type=jnp.float32)]
    all_gather x1 -> x0, local copies, waits for them, and re-layouts: 3.93 us -> none  [per_device(): whole_kv = lax.all_gather(owned_kv, 'seq', axis=0, tiled=True)]
  transfers between devices with their start and end apart: 4 -> 0, of which waited for: 2 -> 0; matrix products, arithmetic and copies ran while one was open for 45% -> 0% of each run, Pallas kernels for 0% -> 0%
where the time goes in v3:
time: 58.3 us; the launch traced here: 58.1 us
  Pallas kernels  55.8 us (96%)
  local copies, waits for them, and re-layouts  2.26 us (4%)
    pallas_call x1, Pallas kernels, per_device(): pl.pallas_call(kernel, name='joining_layer', out_shape=jax.ShapeDtypeStru...  55.8 us
    unnamed x1, local copies, waits for them, and re-layouts  2.26 us

profile of v3, /device:TPU:0, one launch (start us, length us, event | category | flops | bytes accessed | tf_op | source)
XLA Modules:
  0.0 58.1 jit_solution(10645151831686758629)
XLA Ops:
  0.0 55.8 %joining_layer.1 = bf16[512,1024]{1,0:T(8,128)(2,1)} custom-call(s32[8]{0:T(128)} %owner_ref.1, s32[8]{0:T(128)} %len_ref.1, bf16[512,1024]{1,0:T(8,128)(2,1)} %bitcast.6, f32[1,1024]{1,0:T(1,128)} %bitcast.8, f32[1,1024]{1,0:T(1,128)} %bitcast.9, bf16[8,16,1024]{2,1,0:T(8,128)(2,1)} %bitcast.7, bf16[1024,3072]{1,0:T(8,128)(2,1)} %w_hbm.1, ...), custom_call_target="tpu_custom_call" | custom-call | flops 20000000000 | bytes 16777216 | tf_op jit(solution)/shard_map/joining_layer/pallas_call | solution.py:299
  55.9 2.3 %copy.13 = bf16[1,512,1024]{2,1,0:T(8,128)(2,1)} copy(bf16[1,512,1024]{2,1,0:T(8,128)(2,1)} %bitcast.5) | data formatting | bytes 2097152

commit v4 on v3

--- a/solution.py
+++ b/solution.py
@@ -14,6 +14,7 @@
 V_SHRINK = 2.0 ** -10
 V_GROW = 2.0 ** 10
 CHUNKS = 2
+EXTRA = 16
 MESH = pl.DeviceIdType.MESH
 
 
@@ -57,6 +58,7 @@
     half = D // 2
     pairs = half // PAIR
     step = rows // CHUNKS
+    groups = xn.shape[0]
 
     def load(src, dst, sem):
         copy = pltpu.make_async_copy(src, dst, sem)
@@ -138,27 +140,27 @@
     def project(slot, i, with_q):
         at = pl.ds(i * step, step)
         x = xn[slot, at]
-        key_at = pl.ds(slot * rows + i * step, step)
+        start = slot * rows + i * step if slot < 2 else 2 * (rows + i * step) + (slot - 2) * step
+        key_at = pl.ds(start, step)
         if with_q:
             qf = (dot(x, wbuf[0]) * Q_SCALE).astype(jnp.bfloat16)
             for p in range(pairs):
                 q_s[p, key_at] = qf[:, p * PAIR:(p + 1) * PAIR]
         kf = dot(x, wbuf[1])
-        vf = dot(x, wbuf[2]) * V_SHRINK
+        vt = jnp.transpose(dot(x, wbuf[2]) * V_SHRINK).astype(jnp.bfloat16)
         for p in range(pairs):
             kp = kf[:, p * PAIR:(p + 1) * PAIR]
-            vp = vf[:, p * PAIR:(p + 1) * PAIR]
             k_s[2 * p, key_at] = jnp.where(low, kp, 0.0).astype(jnp.bfloat16)
             k_s[2 * p + 1, key_at] = jnp.where(low, 0.0, kp).astype(jnp.bfloat16)
-            v_s[2 * p, key_at] = jnp.where(low, vp, 1.0).astype(jnp.bfloat16)
-            v_s[2 * p + 1, key_at] = jnp.where(low, 1.0, vp).astype(jnp.bfloat16)
-
-    def piece(p, h, q_at, key_at):
-        w = jnp.exp2(dot_nt(q_s[p, q_at], k_s[2 * p + h, key_at])).astype(jnp.bfloat16)
-        return dot(w, v_s[2 * p + h, key_at])
-
-    every = pl.ds(0, 2 * rows)
-
+        for h in range(2 * pairs):
+            v_s[h, :HEAD_DIM, key_at] = vt[h * HEAD_DIM:(h + 1) * HEAD_DIM]
+
+    def piece(p, h, key_at):
+        w = jnp.exp2(dot_nt(k_s[2 * p + h, key_at], q_s[p])).astype(jnp.bfloat16)
+        return dot(v_s[2 * p + h, :, key_at], w)
+
+    for h in range(2 * pairs):
+        v_s[h, HEAD_DIM:] = jnp.ones((EXTRA, groups * rows), jnp.bfloat16)
     for i in range(CHUNKS):
         project(0, i, True)
 
@@ -178,9 +180,7 @@
 
     def local(p):
         for h in range(2):
-            acc[2 * p + h] = piece(p, h, every, pl.ds(0, rows))
-        for h in range(2):
-            acc[2 * p + h] += piece(p, h, every, pl.ds(rows, rows))
+            acc[2 * p + h] = piece(p, h, pl.ds(0, rows)) + piece(p, h, pl.ds(rows, rows))
 
     pl.loop(0, pairs // 2)(local)
 
@@ -207,21 +207,21 @@
                     eq_fwd = push(theirs, theirs, eq_send.at[2], eq_recv.at[2], sib)
                 forwards[i].wait_recv()
             project(slot, i, False)
-            key_at = pl.ds(slot * rows + i * step, step)
-            if slot == 3 and i == CHUNKS - 1:
-                break
-
-            @pl.loop(0, pairs)
-            def _(p):
-                for h in range(2):
-                    acc[2 * p + h] += piece(p, h, every, key_at)
+        key_at = pl.ds(2 * (rows + i * step), 2 * step)
+
+        @pl.loop(0, pairs)
+        def _(p):
+            for h in range(2):
+                acc[2 * p + h] += piece(p, h, key_at)
 
     qlow = low_lanes(rows)
 
     def last(p, q_at):
-        even = acc[2 * p, q_at] + piece(p, 0, q_at, key_at)
-        odd = acc[2 * p + 1, q_at] + piece(p, 1, q_at, key_at)
-        return finish(even, odd, qlow)
+        parts = []
+        for h in range(2):
+            total = acc[2 * p + h, HEAD_DIM:HEAD_DIM + 1, q_at]
+            parts.append(acc[2 * p + h, :HEAD_DIM, q_at] * (V_GROW / total))
+        return jnp.transpose(jnp.concatenate(parts, axis=0)).astype(jnp.bfloat16)
 
     for p in range(pairs):
         away[:, p * PAIR:(p + 1) * PAIR] = last(p, pl.ds(rows, rows))
@@ -308,8 +308,8 @@
             bf16(groups, rows, D),
             bf16(half // PAIR, 2 * rows, PAIR),
             bf16(half // HEAD_DIM, groups * rows, PAIR),
-            bf16(half // HEAD_DIM, groups * rows, PAIR),
-            f32(half // HEAD_DIM, 2 * rows, PAIR),
+            bf16(half // HEAD_DIM, HEAD_DIM + EXTRA, groups * rows),
+            f32(half // HEAD_DIM, HEAD_DIM + EXTRA, 2 * rows),
             bf16(rows, half), bf16(2, rows, half),
             bf16(*pieces.shape), bf16(*pieces.shape), bf16(groups, *pieces.shape),
             bf16(HEADS // 2, rows, PAIR), bf16(keys, 2 * D), f32(rows, D), bf16(rows, D),

time: 58.3 us -> 57.9 us (level)
  no operation moved by 1% of the time
where the time goes in v4:
time: 57.9 us; the launch traced here: 57.7 us
  Pallas kernels  55.5 us (96%)
  local copies, waits for them, and re-layouts  2.26 us (4%)
    pallas_call x1, Pallas kernels, per_device(): pl.pallas_call(kernel, name='joining_layer', out_shape=jax.ShapeDtypeStru...  55.5 us
    unnamed x1, local copies, waits for them, and re-layouts  2.26 us

profile of v4, /device:TPU:0, one launch (start us, length us, event | category | flops | bytes accessed | tf_op | source)
XLA Modules:
  0.0 57.7 jit_solution(3826463832080397682)
XLA Ops:
  0.0 55.5 %joining_layer.1 = bf16[512,1024]{1,0:T(8,128)(2,1)} custom-call(s32[8]{0:T(128)} %owner_ref.1, s32[8]{0:T(128)} %len_ref.1, bf16[512,1024]{1,0:T(8,128)(2,1)} %bitcast.6, f32[1,1024]{1,0:T(1,128)} %bitcast.8, f32[1,1024]{1,0:T(1,128)} %bitcast.9, bf16[8,16,1024]{2,1,0:T(8,128)(2,1)} %bitcast.7, bf16[1024,3072]{1,0:T(8,128)(2,1)} %w_hbm.1, ...), custom_call_target="tpu_custom_call" | custom-call | flops 20000000000 | bytes 16777216 | tf_op jit(solution)/shard_map/joining_layer/pallas_call | solution.py:299
  55.5 2.3 %copy.13 = bf16[1,512,1024]{2,1,0:T(8,128)(2,1)} copy(bf16[1,512,1024]{2,1,0:T(8,128)(2,1)} %bitcast.5) | data formatting | bytes 2097152
